TPU v7x, 32 devices: a whole 2x2x4 slice. The times are simulated.
32 devices in a mesh: dp: 16 (over z, y, core), tensor: 2 (over x).
Axes of the slice: x: 2, y: 2, z: 4, core: 2. Of those that a mesh axis runs over, the one named last changes fastest.
Arguments:
- block_input: bfloat16 [16384, 1536], P('dp'), may hold values from -50 to 50
- cotangent: bfloat16 [16384, 1536], P('dp'), may hold values from -6 to 6
- pre_gain: float32 [1536], replicated, may hold values from 0.5 to 1.5
- gate_proj: bfloat16 [1536, 3072], P(None, 'tensor'), may hold values from -0.15625 to 0.15625
- value_proj: bfloat16 [1536, 3072], P(None, 'tensor'), may hold values from -0.15625 to 0.15625
- step_proj: bfloat16 [1536, 48], P(None, 'tensor'), may hold values from -0.15625 to 0.15625
- state_proj: bfloat16 [1536, 256], replicated, may hold values from -0.15625 to 0.15625
- conv_value: float32 [4, 3072], P(None, 'tensor'), may hold values from -3 to 3
- conv_value_bias: float32 [3072], P('tensor'), may hold values from -3 to 3
- conv_state: float32 [4, 256], replicated, may hold values from -3 to 3
- conv_state_bias: float32 [256], replicated, may hold values from -3 to 3
- step_bias: float32 [48], P('tensor'), may hold values from -6.9 to -2.3
- decay_log: float32 [48], P('tensor'), may hold values from 0 to 2.77
- skip_gain: float32 [48], P('tensor'), may hold values from 0.5 to 1.5
- norm_gain: float32 [3072], P('tensor'), may hold values from 0.5 to 1.5
- out_proj: bfloat16 [3072, 1536], P('tensor'), may hold values from -0.109375 to 0.109375
Outputs:
- block_out: bfloat16 [16384, 1536], P('dp')
- grad_input: float32 [16384, 1536], P('dp')
- grad_pre_gain: float32 [1536], replicated
- grad_gate_proj: float32 [1536, 3072], P(None, 'tensor')
- grad_value_proj: float32 [1536, 3072], P(None, 'tensor')
- grad_step_proj: float32 [1536, 48], P(None, 'tensor')
- grad_state_proj: float32 [1536, 256], replicated
- grad_conv_value: float32 [4, 3072], P(None, 'tensor')
- grad_conv_value_bias: float32 [3072], P('tensor')
- grad_conv_state: float32 [4, 256], replicated
- grad_conv_state_bias: float32 [256], replicated
- grad_step_bias: float32 [48], P('tensor')
- grad_decay_log: float32 [48], P('tensor')
- grad_skip_gain: float32 [48], P('tensor')
- grad_norm_gain: float32 [3072], P('tensor')
- grad_out_proj: float32 [3072, 1536], P('tensor')
All inputs are finite; a program needn't handle non-finite values.
Results may differ from a plain program's by a relative error of at most 0.008.
Values may be sent and summed in bfloat16 or wider, within the bound.
No kernel may reach another device: no remote copies, remote signals or barrier semaphores. Data moves between devices by JAX's collectives and lax.ppermute only.
A program may use at most 256 MiB of HBM per device.

v0:
```python
import jax
import jax.numpy as jnp
from jax import lax
from jax.sharding import PartitionSpec as P

D = 1536
BLOCK = 256
SEQ_LEN = 1024
INNER = 3072


epsilon = 1e-05
highest = lax.Precision.HIGHEST


def causal_conv(values, kernel, offset):
    kernel_width = kernel.shape[0]
    length = values.shape[0]
    padded = jnp.concatenate(
        [jnp.zeros((kernel_width - 1, values.shape[1]), jnp.float32), values], axis=0
    )
    running_sum = jnp.zeros_like(values) + offset[None, :]
    for tap_index in range(kernel_width):
        running_sum = (
            running_sum + kernel[tap_index][None, :] * padded[tap_index : tap_index + length]
        )
    return running_sum


def make_states(bc_raw, conv_state, conv_state_bias):
    return jax.nn.silu(causal_conv(bc_raw, conv_state, conv_state_bias))


def mixer(
    conv_in,
    states,
    step_raw,
    gate_raw,
    conv_value,
    conv_value_bias,
    step_bias,
    decay_log,
    skip_gain,
):
    length = conv_in.shape[0]
    head_count = skip_gain.shape[0]
    head_width = conv_in.shape[1] // head_count
    state_width = states.shape[1] // 2
    block_count = length // BLOCK
    conv_out = jax.nn.silu(causal_conv(conv_in, conv_value, conv_value_bias))
    step_size = jax.nn.softplus(step_raw + step_bias[None, :])
    decay_rate = -jnp.exp(decay_log)
    log_decay = step_size * decay_rate[None, :]
    writer = states[:, :state_width].reshape(block_count, BLOCK, state_width)
    reader = states[:, state_width:].reshape(block_count, BLOCK, state_width)
    head_values = conv_out.reshape(block_count, BLOCK, head_count, head_width)
    cumulative = jnp.cumsum(log_decay.reshape(block_count, BLOCK, head_count), axis=1)
    cum_heads = jnp.transpose(cumulative, (0, 2, 1))
    step_heads = jnp.transpose(step_size.reshape(block_count, BLOCK, head_count), (0, 2, 1))
    scores = jnp.einsum("ktn,ksn->kts", reader, writer, precision=highest)
    causal_mask = jnp.tril(jnp.ones((BLOCK, BLOCK), jnp.float32))
    log_gap = cum_heads[:, :, :, None] - cum_heads[:, :, None, :]
    decay = jnp.exp(jnp.where(causal_mask > 0, log_gap, 0.0)) * causal_mask
    weights = scores[:, None, :, :] * decay * step_heads[:, :, None, :]
    intra_part = jnp.einsum("khts,kshp->kthp", weights, head_values, precision=highest)
    tail_weight = jnp.exp(cum_heads[:, :, -1:] - cum_heads) * step_heads
    block_state = jnp.einsum(
        "ksn,khs,kshp->khnp", writer, tail_weight, head_values, precision=highest
    )
    block_fade = jnp.exp(cum_heads[:, :, -1])

    def advance(carried, item):
        new_part, keep_factor = item
        return (carried * keep_factor[:, None, None] + new_part, carried)

    initial = jnp.zeros((head_count, state_width, head_width), jnp.float32)
    _, entering = lax.scan(advance, initial, (block_state, block_fade))
    inter_part = (
        jnp.einsum("ktn,khnp->kthp", reader, entering, precision=highest)
        * jnp.exp(cumulative)[:, :, :, None]
    )
    mixed_out = intra_part + inter_part + skip_gain[None, None, :, None] * head_values
    mixed_out = mixed_out.reshape(length, head_count * head_width)
    return mixed_out * jax.nn.silu(gate_raw)


def dot_plain(left, right):
    return jnp.dot(left, right, preferred_element_type=jnp.float32)


def dot_inner(left, right):
    return lax.dot_general(
        left, right, (((0,), (0,)), ((), ())), preferred_element_type=jnp.float32
    )


def dot_outer(left, right):
    return lax.dot_general(
        left, right, (((1,), (1,)), ((), ())), preferred_element_type=jnp.float32
    )


def local(
    block_input,
    cotangent,
    pre_gain,
    gate_proj,
    value_proj,
    step_proj,
    state_proj,
    conv_value,
    conv_value_bias,
    conv_state,
    conv_state_bias,
    step_bias,
    decay_log,
    skip_gain,
    norm_gain,
    out_proj,
):
    row_count = block_input.shape[0]
    seq_count = row_count // SEQ_LEN

    def by_sequence(array):
        return array.reshape(seq_count, SEQ_LEN, array.shape[1])

    def by_row(array):
        return array.reshape(row_count, array.shape[2])

    input_f32 = block_input.astype(jnp.float32)
    pre_scale = lax.rsqrt(jnp.mean(input_f32 * input_f32, axis=1, keepdims=True) + epsilon)
    normed = (input_f32 * pre_scale * pre_gain[None, :]).astype(jnp.bfloat16)
    gate_raw = dot_plain(normed, gate_proj)
    conv_in = dot_plain(normed, value_proj)
    step_raw = dot_plain(normed, step_proj)
    bc_raw = dot_plain(normed, state_proj)
    states, state_back = jax.vjp(
        jax.vmap(make_states, in_axes=(0, None, None)),
        by_sequence(bc_raw),
        conv_state,
        conv_state_bias,
    )
    gated_seq, mixer_back = jax.vjp(
        jax.vmap(mixer, in_axes=(0, 0, 0, 0, None, None, None, None, None)),
        by_sequence(conv_in),
        states,
        by_sequence(step_raw),
        by_sequence(gate_raw),
        conv_value,
        conv_value_bias,
        step_bias,
        decay_log,
        skip_gain,
    )
    gated = by_row(gated_seq)
    square_sum = lax.psum(jnp.sum(gated * gated, axis=1), "tensor")
    gate_scale = lax.rsqrt(square_sum[:, None] / INNER + epsilon)
    gated_normed = (gated * gate_scale * norm_gain[None, :]).astype(jnp.bfloat16)
    branch = lax.psum(dot_plain(gated_normed, out_proj).astype(jnp.bfloat16), "tensor").astype(
        jnp.float32
    )
    block_out = (input_f32 + branch).astype(jnp.bfloat16)
    d_gn = dot_outer(cotangent, out_proj)
    grad_out_proj = dot_inner(gated_normed, cotangent)
    grad_norm_gain = jnp.sum(d_gn * gated * gate_scale, axis=0)
    gate_dot = lax.psum(jnp.sum(d_gn * norm_gain[None, :] * gated, axis=1), "tensor")
    d_gated = (
        gate_scale * norm_gain[None, :] * d_gn - gated * gate_scale**3 * gate_dot[:, None] / INNER
    )
    (
        d_conv_in,
        d_states,
        d_step_raw,
        d_gate_raw,
        grad_conv_value,
        grad_conv_value_bias,
        grad_step_bias,
        grad_decay_log,
        grad_skip_gain,
    ) = mixer_back(by_sequence(d_gated))
    state_total = lax.psum(by_row(d_states), "tensor")
    d_bc_raw, grad_conv_state, grad_conv_state_bias = state_back(by_sequence(state_total))
    gate_bf = by_row(d_gate_raw).astype(jnp.bfloat16)
    value_bf = by_row(d_conv_in).astype(jnp.bfloat16)
    step_bf = by_row(d_step_raw).astype(jnp.bfloat16)
    state_bf = by_row(d_bc_raw).astype(jnp.bfloat16)
    head_terms = (
        dot_outer(gate_bf, gate_proj)
        + dot_outer(value_bf, value_proj)
        + dot_outer(step_bf, step_proj)
    )
    d_normed = lax.psum(head_terms, "tensor") + dot_outer(state_bf, state_proj)
    grad_pre_gain = jnp.sum(d_normed * input_f32 * pre_scale, axis=0)
    pre_dot = jnp.sum(d_normed * pre_gain[None, :] * input_f32, axis=1, keepdims=True)
    grad_input = (
        cotangent.astype(jnp.float32)
        + pre_scale * pre_gain[None, :] * d_normed
        - input_f32 * pre_scale**3 * pre_dot / D
    )
    grad_gate_proj = dot_inner(normed, gate_bf)
    grad_value_proj = dot_inner(normed, value_bf)
    grad_step_proj = dot_inner(normed, step_bf)
    grad_state_proj = dot_inner(normed, state_bf)
    (
        grad_pre_gain,
        grad_gate_proj,
        grad_value_proj,
        grad_step_proj,
        grad_state_proj,
        grad_conv_value,
        grad_conv_value_bias,
        grad_conv_state,
        grad_conv_state_bias,
        grad_step_bias,
        grad_decay_log,
        grad_skip_gain,
        grad_norm_gain,
        grad_out_proj,
    ) = lax.psum(
        (
            grad_pre_gain,
            grad_gate_proj,
            grad_value_proj,
            grad_step_proj,
            grad_state_proj,
            grad_conv_value,
            grad_conv_value_bias,
            grad_conv_state,
            grad_conv_state_bias,
            grad_step_bias,
            grad_decay_log,
            grad_skip_gain,
            grad_norm_gain,
            grad_out_proj,
        ),
        "dp",
    )
    return (
        block_out,
        grad_input,
        grad_pre_gain,
        grad_gate_proj,
        grad_value_proj,
        grad_step_proj,
        grad_state_proj,
        grad_conv_value,
        grad_conv_value_bias,
        grad_conv_state,
        grad_conv_state_bias,
        grad_step_bias,
        grad_decay_log,
        grad_skip_gain,
        grad_norm_gain,
        grad_out_proj,
    )


def solution(mesh):
    placed = (
        P("dp", None),
        P("dp", None),
        P(),
        P(None, "tensor"),
        P(None, "tensor"),
        P(None, "tensor"),
        P(),
        P(None, "tensor"),
        P("tensor"),
        P(),
        P(),
        P("tensor"),
        P("tensor"),
        P("tensor"),
        P("tensor"),
        P("tensor", None),
    )
    return jax.shard_map(
        local,
        mesh=mesh,
        in_specs=placed,
        out_specs=(
            P("dp", None),
            P("dp", None),
            P(),
            P(None, "tensor"),
            P(None, "tensor"),
            P(None, "tensor"),
            P(),
            P(None, "tensor"),
            P("tensor"),
            P(),
            P(),
            P("tensor"),
            P("tensor"),
            P("tensor"),
            P("tensor"),
            P("tensor", None),
        ),
        check_vma=False,
    )
```

profile of v0, /device:TPU:0, one launch (start us, length us, event | category | flops | bytes accessed | tf_op | source)
XLA Modules:
  0.0 1340.4 jit_solution(6802195912920558726)
XLA Ops:
  9.3 2.6 fusion.31
  13.1 2.7 fusion.33
  21.9 7.8 fusion.139
  29.8 6.5 fusion.49
  36.3 6.6 copy.193
  42.9 10.0 reshape.687
  56.0 2.9 fusion.140
  62.4 8.3 reshape.642
  71.3 10.3 fusion.83
  81.6 3.5 broadcast.218.clone
  85.1 23.3 %while.34 = (s32[]{:T(128)}, f32[1,24,128,64]{3,2,1,0:T(8,128)S(1)}, f32[4,1,24,128,64]{4,3,2,1,0:T(8,128)}, f32[4,1,24,1,1]{2,4,3,1,0:T(1,128)S(1)}, f32[4,1,24...) while((s32[]{:T(128)}, f32[1,24,128,64]{3,2,1,0:T(8,128)S(1)}, ...), condition=%wide.region_4.5_spmd.clone, body=%wide.region_3.4_spmd.clone.sunk | while | flops 786435 | bytes 7865752 | solution.py:77
  108.4 6.2 copy.205
  115.6 8.7 fusion.142
  124.4 9.8 copy.207
  134.3 33.3 %fusion.42 = f32[1,4,256,24,64]{2,4,3,1,0:T(8,128)} fusion(f32[1,4,256,24,64]{2,4,3,1,0:T(8,128)} %copy.207, f32[4,256,24,64]{1,3,2,0:T(8,128)} %bitcast.279, f32[24]{0:T(128)S(1)} %copy-done.93, f32[4,256,24]{1,2,0:T(8,128)S(1)} %bitcast.300, f32[4,24,256]{2,1,0:T(8,128)S(1)} %copy-done.48, f32[256,256]{1,0:T(8,128)S(1)} %copy-done.42, ...), kind=kOutput, calls=%fused_computation.68 | convolution fusion | flops 4869586944 | bytes 26837088 | tf_op jit(solution)/shard_map/jvp(vmap(khts,kshp->kthp))/dot_general | solution.py:65
  167.6 9.8 copy.254
  177.3 11.1 reshape.688
  188.4 12.5 multiply_reduce_fusion.10
  200.9 5.8 psum.133
  206.8 11.6 multiply_reduce_fusion.3
  218.4 4.9 psum.135
  223.3 11.5 fusion.28
  238.1 9.1 fusion.43
  247.1 6.6 copy.211
  253.7 8.1 reshape.659
  261.8 8.4 reshape.662
  270.3 7.4 multiply_reduce_fusion.8
  278.0 20.9 %fusion.89 = f32[4,256,128]{2,1,0:T(8,128)} fusion(f32[4,256,24,64]{1,0,3,2:T(4,128)S(1)} %copy-done.3, f32[4,256,24]{1,2,0:T(8,128)S(1)} %bitcast.301, f32[4,1,24,128,64]{4,3,2,1,0:T(8,128)S(1)} %bitcast.268), kind=kOutput, calls=%fused_computation.126 | convolution fusion | flops 2417491968 | bytes 10059776 | tf_op jit(solution)/shard_map/transpose(jvp(vmap(ktn,khnp->kthp)))/dot_general | solution.py:79
  299.0 45.9 %fusion.11 = (f32[4,24,256]{2,1,0:T(8,128)}, f32[4,24,256]{2,1,0:T(8,128)}, f32[4,24,256]{2,1,0:T(8,128)}, f32[4,256,256]{2,1,0:T(8,128)}) fusion(f32[4,24,256]{2,1,0:T(8,128)S(1)} %copy-done.49, f32[256,256]{1,0:T(8,128)S(1)} %copy-done.43, f32[4,24,256]{2,1,0:T(8,128)S(1)} %copy-done.52, f32[4,256,256]{2,1,0:T(8,128)S(1)} %copy-done.32, ...), kind=kOutput, calls=%fused_computation.30 | convolution fusion | flops 4925874176 | bytes 15499264 | tf_op jit(solution)/shard_map/transpose(jvp(vmap(khts,kshp->kthp)))/dot_general | solution.py:65
  344.9 7.7 fusion.86
  352.5 3.5 broadcast.218
  356.0 26.0 %while.35 = (s32[]{:T(128)}, f32[1,24,128,64]{3,2,1,0:T(8,128)S(1)}, f32[4,1,24,128,64]{4,3,2,1,0:T(8,128)}, f32[4,1,24]{2,1,0:T(1,128)S(1)}, f32[4,1,24,128,64]...) while((s32[]{:T(128)}, ...), condition=%wide.region_12.13_spmd.clone, body=%wide.region_10.12_spmd.clone.sunk | while | flops 1179628 | bytes 8652312 | solution.py:77
  360.3 2.4 fusion.192
  366.8 2.4 fusion.192
  373.2 2.4 fusion.192
  379.7 2.4 fusion.192
  382.2 12.6 fusion.80
  394.8 2.7 copy-done.7
  397.5 27.4 %bitcast_add_fusion.2 = f32[1,4,256,24,64]{2,4,3,1,0:T(8,128)} fusion(f32[4,256,24,64]{1,3,2,0:T(8,128)S(1)} %fusion.80, f32[4,256,24,64]{1,0,3,2:T(4,128)} %reshape.659, f32[24]{0:T(128)S(1)} %copy-done.93, f32[4,256,24]{1,2,0:T(8,128)S(1)} %copy-done.35, f32[4,24,256]{2,1,0:T(8,128)S(1)} %copy-done.50, f32[256,256]{1,0:T(8,128)S(1)} %copy-done.44, ...), kind=kOutput, calls=%fused_computation.66 | convolution fusion | flops 4869586944 | bytes 26837088 | tf_op jit(solution)/shard_map/transpose(jvp(vmap(khts,kshp->kthp)))/dot_general | solution.py:65
  425.0 10.1 multiply_reduce_fusion.2
  437.5 6.6 fusion.97
  445.9 10.0 reduce-window.16
  456.6 9.8 copy.256
  466.3 11.1 reshape.689
  477.5 14.4 %multiply_reduce_fusion.6 = (f32[1536]{0:T(1024)S(1)}, f32[1536]{0:T(1024)S(1)}, f32[1536]{0:T(1024)S(1)}, f32[1536]{0:T(1024)S(1)}, f32[1536]{0:T(1024)S(1)}, /*index=5*/f32[1,1024,1536]{2,1,0:T(8,128)S(1)}) fusion(f32[1,1024,1536]{2,1,0:T(8,128)} %bitcast.270, f32[1024,1536]{1,0:T(8,128)} %copy-done.2, f32[1,1024,1536]{2,1,0:T(8,128)} %get-tuple-element.386, ...), kind=kLoop, calls=%fused_computation.80 | loop fusion | flops 28303872 | bytes 31488000 | tf_op jit(solution)/shard_map/transpose(jvp(vmap()))/reduce_sum | solution.py:25
  492.0 9.3 fusion.143
  501.3 6.0 broadcast_multiply_fusion
  507.2 6.3 fusion.66
  513.6 8.1 fusion.144
  523.1 3.7 add_add_fusion
  527.5 9.9 convolution_convert_fusion
  537.5 3.1 fusion.115
  540.6 10.4 fusion.145
  551.0 7.6 fusion.146
  558.7 7.9 fusion.128
  566.6 138.1 %all-reduce.33.cloned.1.call-done = (f32[1024,1536]{1,0:T(8,128)}, f32[1,1024,256]{2,1,0:T(8,128)}) async-done(((f32[1024,1536]{1,0:T(8,128)}, f32[1,1024,256]{2,1,0:T(8,128)}), (f32[1024,1536]{1,0:T(8,128)}, f32[1,1024,256]{2,1,0:T(8,128)})) %all-reduce.33.cloned.1.call-update) | async-done | bytes 7340048 | tf_op jit(solution)/shard_map/psum | solution.py:192
  711.9 7.3 fusion.40
  719.2 62.5 %all-reduce.22 = (f32[1536]{0:T(1024)}, f32[4,1536]{1,0:T(4,128)}, f32[1536]{0:T(1024)}, f32[4,256]{1,0:T(4,128)}, f32[256]{0:T(256)}, /*index=5*/f32[24]{0:T(128)}, f32[24]{0:T(128)}, f32[24]{0:T(128)}, f32[1536]{0:T(1024)}) all-reduce(f32[1536]{0:T(1024)S(1)} %get-tuple-element.314, ...), channel_id=1, replica_groups=mesh['dp'=16,'tensor'=2] {'dp'}, use_global_device_ids=true, to_apply=%region_25.26 | all-reduce | flops 12104 | bytes 96832 | tf_op jit(solution)/shard_map/psum | solution.py:219
  781.6 11.2 all-reduce.29.cloned.1.call-done
  792.9 9.0 fusion.37
  801.9 509.1 %all-reduce.31.cloned.1.call-done = (f32[1536,1536]{1,0:T(8,128)}, f32[1536,1536]{1,0:T(8,128)}, f32[1536,24]{0,1:T(8,128)}, f32[1536,256]{1,0:T(8,128)}, f32[1536,1536]{1,0:T(8,128)}) async-done(((f32[1536,1536]{1,0:T(8,128)}, f32[1536,1536]{1,0:T(8,128)}, f32[1536,24]{0,1:T(8,128)}, f32[1536,256]{1,0:T(8,128)}, f32[1536,1536]{1,0:T(8,128)}), (f32[1536,1536]{1,0:T(8,128)}, f32[1536,1536]{1,0:T(8,128)}, ...) | async-done | bytes 30031888 | tf_op jit(solution)/shard_map/psum | solution.py:219
  1311.0 8.5 copy.367
  1319.4 8.4 copy.368
  1329.7 3.7 copy.371
  (351 shorter events, 76.2 us)
Async XLA Ops:
  7.2 48.8 %copy-start = (bf16[1536,256]{1,0:T(8,128)(2,1)S(1)}, bf16[1536,256]{1,0:T(8,128)(2,1)}, u32[]{:S(2)}) copy-start(bf16[1536,256]{1,0:T(8,128)(2,1)} %param.26) | copy-start | bytes 2359300
  7.2 10.2 copy-start.40
  7.2 10.2 copy-start.91
  7.2 697.5 %all-reduce.33.cloned.1.call-start = ((), (), s32[]{:S(2)}) async-start(), calls=%async_computation.2 | async-start | bytes 14680064 | tf_op jit(solution)/shard_map/psum | solution.py:192
  9.3 9.7 copy-start.88
  42.9 10.0 copy-start.90
  71.3 13.8 %copy-start.34 = (f32[4,256,24]{1,2,0:T(8,128)}, f32[4,256,24]{1,2,0:T(8,128)S(1)}, u32[]{:S(2)}) copy-start(f32[4,256,24]{1,2,0:T(8,128)S(1)} %get-tuple-element.417) | copy-start | bytes 294916
  115.6 18.6 %copy-start.31 = (f32[4,256,256]{2,1,0:T(8,128)}, f32[4,256,256]{2,1,0:T(8,128)S(1)}, u32[]{:S(2)}) copy-start(f32[4,256,256]{2,1,0:T(8,128)S(1)} %fusion.141) | copy-start | bytes 3145732
  124.3 9.8 copy-start.38
  124.3 9.8 copy-start.39
  124.3 9.9 copy-start.42
  124.3 9.9 copy-start.48
  124.3 9.9 copy-start.64
  124.4 9.9 copy-start.93
  134.2 33.4 %copy-start.51 = (f32[4,24,256]{2,1,0:T(8,128)}, f32[4,24,256]{2,1,0:T(8,128)S(1)}, u32[]{:S(2)}) copy-start(f32[4,24,256]{2,1,0:T(8,128)S(1)} %reduce_window_sum.55) | copy-start | bytes 294916
  188.4 18.4 %copy-start.71 = (f32[1536]{0:T(1024)S(1)}, f32[1536]{0:T(1024)}, u32[]{:S(2)}) copy-start(f32[1536]{0:T(1024)} %param.34) | copy-start | bytes 18436
  206.8 28.0 %copy-start.69 = (f32[1024]{0:T(1024)}, f32[1024]{0:T(1024)S(1)}, u32[]{:S(2)}) copy-start(f32[1024]{0:T(1024)S(1)} %get-tuple-element.408) | copy-start | bytes 12292
  223.3 11.5 copy-start.8
  223.3 13.0 copy-start.9
  223.3 14.7 %copy-start.10 = (f32[1024,1536]{1,0:T(8,128)S(1)}, f32[1024,1536]{1,0:T(8,128)}, u32[]{:S(2)}) copy-start(f32[1024,1536]{1,0:T(8,128)} %get-tuple-element.415) | copy-start | bytes 18874372
  261.8 15.8 %slice-start = ((s8[6291456]{0:T(1024)(128)(4,1)}), s8[2097152]{0:T(1024)(128)(4,1)S(1)}, s32[]{:S(2)}) async-start(s8[6291456]{0:T(1024)(128)(4,1)} %bitcast.267), calls=%async_computation.3 | async-start | bytes 4194304
  270.3 28.6 %slice-start.2 = ((s8[6291456]{0:T(1024)(128)(4,1)}), s8[2097152]{0:T(1024)(128)(4,1)S(1)}, s32[]{:S(2)}) async-start(s8[6291456]{0:T(1024)(128)(4,1)} %bitcast.271), calls=%async_computation.5 | async-start | bytes 4194304
  277.9 21.0 %slice-start.3 = ((s8[6291456]{0:T(1024)(128)(4,1)}), s8[4194304]{0:T(1024)(128)(4,1)S(1)}, s32[]{:S(2)}) async-start(s8[6291456]{0:T(1024)(128)(4,1)} %bitcast.271), calls=%async_computation.6 | async-start | bytes 8388608
  277.9 21.0 %copy-start.18 = (f32[1,4,256,24,64]{2,1,4,3,0:T(4,128)S(1)}, f32[1,4,256,24,64]{2,1,4,3,0:T(4,128)}, u32[]{:S(2)}) copy-start(f32[1,4,256,24,64]{2,1,4,3,0:T(4,128)} %reshape.662) | copy-start | bytes 18874372
  277.9 21.0 %copy-start.32 = (f32[4,256,256]{2,1,0:T(8,128)S(1)}, f32[4,256,256]{2,1,0:T(8,128)}, u32[]{:S(2)}) copy-start(f32[4,256,256]{2,1,0:T(8,128)} %copy-done.31) | copy-start | bytes 3145732
  277.9 21.0 %copy-start.43 = (f32[256,256]{1,0:T(8,128)S(1)}, f32[256,256]{1,0:T(8,128)}, u32[]{:S(2)}) copy-start(f32[256,256]{1,0:T(8,128)} %fusion.108) | copy-start | bytes 786436
  277.9 21.0 %copy-start.49 = (f32[4,24,256]{2,1,0:T(8,128)S(1)}, f32[4,24,256]{2,1,0:T(8,128)}, u32[]{:S(2)}) copy-start(f32[4,24,256]{2,1,0:T(8,128)} %get-tuple-element.418) | copy-start | bytes 294916
  277.9 21.0 %copy-start.52 = (f32[4,24,256]{2,1,0:T(8,128)S(1)}, f32[4,24,256]{2,1,0:T(8,128)}, u32[]{:S(2)}) copy-start(f32[4,24,256]{2,1,0:T(8,128)} %copy-done.51) | copy-start | bytes 294916
  277.9 21.0 %copy-start.65 = (pred[256,256]{1,0:T(8,128)(4,1)S(1)}, pred[256,256]{1,0:T(8,128)(4,1)}, u32[]{:S(2)}) copy-start(pred[256,256]{1,0:T(8,128)(4,1)} %broadcast_compare_fusion) | copy-start | bytes 196612
  344.9 11.2 copy-start.1
  382.1 15.4 %copy-start.33 = (f32[4,256,256]{2,1,0:T(8,128)S(1)}, f32[4,256,256]{2,1,0:T(8,128)}, u32[]{:S(2)}) copy-start(f32[4,256,256]{2,1,0:T(8,128)} %copy-done.31) | copy-start | bytes 3145732
  382.1 15.4 %copy-start.35 = (f32[4,256,24]{1,2,0:T(8,128)S(1)}, f32[4,256,24]{1,2,0:T(8,128)}, u32[]{:S(2)}) copy-start(f32[4,256,24]{1,2,0:T(8,128)} %copy-done.34) | copy-start | bytes 294916
  382.1 15.4 %copy-start.44 = (f32[256,256]{1,0:T(8,128)S(1)}, f32[256,256]{1,0:T(8,128)}, u32[]{:S(2)}) copy-start(f32[256,256]{1,0:T(8,128)} %fusion.108) | copy-start | bytes 786436
  382.1 15.4 %copy-start.50 = (f32[4,24,256]{2,1,0:T(8,128)S(1)}, f32[4,24,256]{2,1,0:T(8,128)}, u32[]{:S(2)}) copy-start(f32[4,24,256]{2,1,0:T(8,128)} %get-tuple-element.418) | copy-start | bytes 294916
  382.1 15.4 %copy-start.53 = (f32[4,24,256]{2,1,0:T(8,128)S(1)}, f32[4,24,256]{2,1,0:T(8,128)}, u32[]{:S(2)}) copy-start(f32[4,24,256]{2,1,0:T(8,128)} %copy-done.51) | copy-start | bytes 294916
  382.1 15.4 %copy-start.66 = (pred[256,256]{1,0:T(8,128)(4,1)S(1)}, pred[256,256]{1,0:T(8,128)(4,1)}, u32[]{:S(2)}) copy-start(pred[256,256]{1,0:T(8,128)(4,1)} %broadcast_compare_fusion) | copy-start | bytes 196612
  382.1 42.8 %slice-start.4 = ((s8[6291456]{0:T(1024)(128)(4,1)}), s8[4194304]{0:T(1024)(128)(4,1)S(1)}, s32[]{:S(2)}) async-start(s8[6291456]{0:T(1024)(128)(4,1)} %bitcast.273), calls=%async_computation.7 | async-start | bytes 8388608
  382.2 55.2 %slice-start.6 = ((s8[6291456]{0:T(1024)(128)(4,1)}), s8[4194304]{0:T(1024)(128)(4,1)S(1)}, s32[]{:S(2)}) async-start(s8[6291456]{0:T(1024)(128)(4,1)} %bitcast.275), calls=%async_computation.9 | async-start | bytes 8388608
  397.5 27.5 %slice-start.5 = ((s8[6291456]{0:T(1024)(128)(4,1)}), s8[2097152]{0:T(1024)(128)(4,1)S(1)}, s32[]{:S(2)}) async-start(s8[6291456]{0:T(1024)(128)(4,1)} %bitcast.273), calls=%async_computation.8 | async-start | bytes 4194304
  397.5 39.9 %slice-start.7 = ((s8[6291456]{0:T(1024)(128)(4,1)}), s8[2097152]{0:T(1024)(128)(4,1)S(1)}, s32[]{:S(2)}) async-start(s8[6291456]{0:T(1024)(128)(4,1)} %bitcast.275), calls=%async_computation.10 | async-start | bytes 4194304
  425.0 10.1 copy-start.17
  425.0 10.1 copy-start.20
  425.0 11.3 copy-start.15
  425.0 11.3 copy-start.27
  425.0 12.3 copy-start.47
  477.5 14.5 %copy-start.22 = (bf16[1024,1536]{1,0:T(8,128)(2,1)S(1)}, bf16[1024,1536]{1,0:T(8,128)(2,1)}, u32[]{:S(2)}) copy-start(bf16[1024,1536]{1,0:T(8,128)(2,1)} %fusion.28) | copy-start | bytes 9437188
  507.2 15.8 %slice-start.13 = ((s8[6291456]{0:T(1024)(128)(4,1)}), s8[2097152]{0:T(1024)(128)(4,1)S(1)}, s32[]{:S(2)}) async-start(s8[6291456]{0:T(1024)(128)(4,1)} %bitcast.294), calls=%async_computation.16 | async-start | bytes 4194304
  513.6 9.5 slice-start.14
  513.6 9.4 copy-start.41
  526.8 266.0 %all-reduce.29.cloned.1.call-start = ((), (), s32[]{:S(2)}) async-start(), calls=%async_computation | async-start | bytes 6291456 | tf_op jit(solution)/shard_map/psum | solution.py:159
  537.5 773.5 %all-reduce.31.cloned.1.call-start = ((), (), s32[]{:S(2)}) async-start(), calls=%async_computation.1 | async-start | bytes 60063744 | tf_op jit(solution)/shard_map/psum | solution.py:219
  540.6 10.4 copy-start.5
  540.6 10.4 copy-start.24
  540.6 18.0 %slice-start.8 = ((s8[6291456]{0:T(1024)(128)(4,1)}), s8[4194304]{0:T(1024)(128)(4,1)S(1)}, s32[]{:S(2)}) async-start(s8[6291456]{0:T(1024)(128)(4,1)} %bitcast.277), calls=%async_computation.11 | async-start | bytes 8388608
  558.6 146.0 %copy-start.12 = (f32[1024,256]{1,0:T(8,128)S(1)}, f32[1024,256]{1,0:T(8,128)}, u32[]{:S(2)}) copy-start(f32[1024,256]{1,0:T(8,128)} %copy-done.11) | copy-start | bytes 3145732
  558.7 146.0 %copy-start.19 = (f32[1,1024,256]{2,1,0:T(8,128)S(1)}, f32[1,1024,256]{2,1,0:T(8,128)}, u32[]{:S(2)}) copy-start(f32[1,1024,256]{2,1,0:T(8,128)} %get-tuple-element.384) | copy-start | bytes 3145732
  558.7 148.1 %copy-start.79 = (f32[1,256]{1,0:T(1,128)S(1)}, f32[1,256]{1,0:T(1,128)}, u32[]{:S(2)}) copy-start(f32[1,256]{1,0:T(1,128)} %copy-done.78) | copy-start | bytes 3076
  558.7 148.1 %copy-start.81 = (f32[1,256]{1,0:T(1,128)S(1)}, f32[1,256]{1,0:T(1,128)}, u32[]{:S(2)}) copy-start(f32[1,256]{1,0:T(1,128)} %copy-done.80) | copy-start | bytes 3076
  558.7 148.1 %copy-start.83 = (f32[1,256]{1,0:T(1,128)S(1)}, f32[1,256]{1,0:T(1,128)}, u32[]{:S(2)}) copy-start(f32[1,256]{1,0:T(1,128)} %copy-done.82) | copy-start | bytes 3076
  558.7 148.1 %copy-start.85 = (f32[1,256]{1,0:T(1,128)S(1)}, f32[1,256]{1,0:T(1,128)}, u32[]{:S(2)}) copy-start(f32[1,256]{1,0:T(1,128)} %copy-done.84) | copy-start | bytes 3076
  711.9 81.0 %copy-start.77 = (f32[1024]{0:T(1024)S(1)}, f32[1024]{0:T(1024)}, u32[]{:S(2)}) copy-start(f32[1024]{0:T(1024)} %get-tuple-element.405) | copy-start | bytes 12292
  1311.0 18.7 %slice-start.10 = ((s8[9437184]{0:T(1024)(128)(4,1)}), s8[4194304]{0:T(1024)(128)(4,1)S(1)}, s32[]{:S(2)}) async-start(s8[9437184]{0:T(1024)(128)(4,1)} %bitcast.292), calls=%async_computation.13 | async-start | bytes 8388608
  1311.0 18.7 %slice-start.11 = ((s8[9437184]{0:T(1024)(128)(4,1)}), s8[4194304]{0:T(1024)(128)(4,1)S(1)}, s32[]{:S(2)}) async-start(s8[9437184]{0:T(1024)(128)(4,1)} %bitcast.292), calls=%async_computation.14 | async-start | bytes 8388608
  1319.4 10.2 slice-start.12
  (49 other events, 308.7 us)
Sparse Core Ops, SparseCore 0:
  526.9 177.7 all-reduce.32
  707.0 85.8 all-reduce.28
  799.3 511.6 all-reduce.30
where the time goes:
time: 1350 us; the launch traced here: 1340 us
  waiting for transfers between devices  658 us (49%)
  matrix products  283 us (21%)
  local copies, waits for them, and re-layouts  176 us (13%)
  other arithmetic  134 us (10%)
  blocking collectives  73.2 us (5%)
  between operations  15.7 us (1%)
    psum x1, waiting for transfers between devices, local(): lax.psum((grad_pre_gain, grad_gate_proj, grad_value_proj, grad_step_proj,...  509 us
    psum x1, waiting for transfers between devices, local(): d_normed = lax.psum(head_terms, 'tensor') + dot_outer(state_bf, state_proj)  138 us
    dot_general x3, matrix products, mixer(): jnp.einsum('khts,kshp->kthp', weights, head_values, precision=highest)  107 us
    psum x1, blocking collectives, local(): lax.psum((grad_pre_gain, grad_gate_proj, grad_value_proj, grad_step_proj,...  62.5 us
    reshape x4, local copies, waits for them, and re-layouts, mixer(): head_values = conv_out.reshape(block_count, BLOCK, head_count, head_width)  40.7 us
    dot_general x5, matrix products, dot_outer(): lax.dot_general(left, right, (((1,), (1,)), ((), ())), preferred_element_...  40 us
    reshape x4, local copies, waits for them, and re-layouts, mixer(): mixed_out = mixed_out.reshape(length, head_count * head_width)  37.4 us
    unnamed x228, local copies, waits for them, and re-layouts  34.9 us
  transfers between devices with their start and end apart: 3, of which 3 were waited for; matrix products, arithmetic and copies ran while one was open for 5% of the time, Pallas kernels for 0%

commit v1 on v0

--- a/solution.py
+++ b/solution.py
@@ -153,20 +153,23 @@
         skip_gain,
     )
     gated = by_row(gated_seq)
-    square_sum = lax.psum(jnp.sum(gated * gated, axis=1), "tensor")
-    gate_scale = lax.rsqrt(square_sum[:, None] / INNER + epsilon)
+    d_gn = dot_outer(cotangent, out_proj)
+    weighted = d_gn * norm_gain[None, :]
+    row_sums = lax.psum(
+        jnp.stack([jnp.sum(gated * gated, axis=1), jnp.sum(weighted * gated, axis=1)]), "tensor"
+    )
+    gate_scale = lax.rsqrt(row_sums[0][:, None] / INNER + epsilon)
+    gate_dot = row_sums[1][:, None]
     gated_normed = (gated * gate_scale * norm_gain[None, :]).astype(jnp.bfloat16)
-    branch = lax.psum(dot_plain(gated_normed, out_proj).astype(jnp.bfloat16), "tensor").astype(
-        jnp.float32
-    )
-    block_out = (input_f32 + branch).astype(jnp.bfloat16)
-    d_gn = dot_outer(cotangent, out_proj)
+    swap = [(0, 1), (1, 0)]
+    branch = dot_plain(gated_normed, out_proj).astype(jnp.bfloat16)
+    branch_other = lax.ppermute(branch, "tensor", swap)
+    block_out = (
+        input_f32 + (branch.astype(jnp.float32) + branch_other.astype(jnp.float32))
+    ).astype(jnp.bfloat16)
     grad_out_proj = dot_inner(gated_normed, cotangent)
     grad_norm_gain = jnp.sum(d_gn * gated * gate_scale, axis=0)
-    gate_dot = lax.psum(jnp.sum(d_gn * norm_gain[None, :] * gated, axis=1), "tensor")
-    d_gated = (
-        gate_scale * norm_gain[None, :] * d_gn - gated * gate_scale**3 * gate_dot[:, None] / INNER
-    )
+    d_gated = gate_scale * weighted - gated * gate_scale**3 * gate_dot / INNER
     (
         d_conv_in,
         d_states,
@@ -178,8 +181,7 @@
         grad_decay_log,
         grad_skip_gain,
     ) = mixer_back(by_sequence(d_gated))
-    state_total = lax.psum(by_row(d_states), "tensor")
-    d_bc_raw, grad_conv_state, grad_conv_state_bias = state_back(by_sequence(state_total))
+    d_bc_raw, grad_conv_state, grad_conv_state_bias = state_back(d_states)
     gate_bf = by_row(d_gate_raw).astype(jnp.bfloat16)
     value_bf = by_row(d_conv_in).astype(jnp.bfloat16)
     step_bf = by_row(d_step_raw).astype(jnp.bfloat16)
@@ -188,50 +190,47 @@
         dot_outer(gate_bf, gate_proj)
         + dot_outer(value_bf, value_proj)
         + dot_outer(step_bf, step_proj)
-    )
-    d_normed = lax.psum(head_terms, "tensor") + dot_outer(state_bf, state_proj)
-    grad_pre_gain = jnp.sum(d_normed * input_f32 * pre_scale, axis=0)
+        + dot_outer(state_bf, state_proj)
+    )
+    grad_pre_gain = jnp.sum(head_terms * input_f32 * pre_scale, axis=0)
+    mine = head_terms.astype(jnp.bfloat16)
+    other = lax.ppermute(mine, "tensor", swap)
+    d_normed = mine.astype(jnp.float32) + other.astype(jnp.float32)
     pre_dot = jnp.sum(d_normed * pre_gain[None, :] * input_f32, axis=1, keepdims=True)
     grad_input = (
         cotangent.astype(jnp.float32)
         + pre_scale * pre_gain[None, :] * d_normed
         - input_f32 * pre_scale**3 * pre_dot / D
     )
-    grad_gate_proj = dot_inner(normed, gate_bf)
-    grad_value_proj = dot_inner(normed, value_bf)
-    grad_step_proj = dot_inner(normed, step_bf)
-    grad_state_proj = dot_inner(normed, state_bf)
+
+    def summed(array):
+        return lax.psum(array.astype(jnp.bfloat16), "dp").astype(jnp.float32)
+
+    grad_out_proj = summed(grad_out_proj)
+    grad_gate_proj = summed(dot_inner(normed, gate_bf))
+    grad_value_proj = summed(dot_inner(normed, value_bf))
+    grad_step_proj = summed(dot_inner(normed, step_bf))
+    grad_state_proj = lax.psum(
+        dot_inner(normed, state_bf).astype(jnp.bfloat16), ("dp", "tensor")
+    ).astype(jnp.float32)
+    grad_pre_gain, grad_conv_state, grad_conv_state_bias = lax.psum(
+        (grad_pre_gain, grad_conv_state, grad_conv_state_bias), ("dp", "tensor")
+    )
     (
-        grad_pre_gain,
-        grad_gate_proj,
-        grad_value_proj,
-        grad_step_proj,
-        grad_state_proj,
         grad_conv_value,
         grad_conv_value_bias,
-        grad_conv_state,
-        grad_conv_state_bias,
         grad_step_bias,
         grad_decay_log,
         grad_skip_gain,
         grad_norm_gain,
-        grad_out_proj,
     ) = lax.psum(
         (
-            grad_pre_gain,
-            grad_gate_proj,
-            grad_value_proj,
-            grad_step_proj,
-            grad_state_proj,
             grad_conv_value,
             grad_conv_value_bias,
-            grad_conv_state,
-            grad_conv_state_bias,
             grad_step_bias,
             grad_decay_log,
             grad_skip_gain,
             grad_norm_gain,
-            grad_out_proj,
         ),
         "dp",
     )

time: 1350 us -> 834 us (0.62)
  waiting for transfers between devices: 658 us -> 52.4 us
  blocking collectives: 73.2 us -> 158 us
  other arithmetic: 134 us -> 168 us
  local copies, waits for them, and re-layouts: 176 us -> 148 us
    psum x3 -> x2, waiting for transfers between devices: 658 us -> 52.3 us  [the longest x1 52.3 us: summed(): return lax.psum(array.astype(jnp.bfloat16), 'dp').astype(jnp.float32)]
    psum x3, blocking collectives: 73.2 us -> 158 us  [the longest x1 87.2 us: local(): lax.psum((grad_pre_gain, grad_conv_state, grad_conv_state_bias), ('dp', '...]
    unnamed x228 -> x203, local copies, waits for them, and re-layouts: 34.9 us -> 7.75 us
    reduce_sum x0 -> x2, other arithmetic: none -> 18.9 us  [the longest x1 11.3 us: local(): grad_norm_gain = jnp.sum(d_gn * gated * gate_scale, axis=0)]
  transfers between devices with their start and end apart: 3 -> 4, of which waited for: 3 -> 1; matrix products, arithmetic and copies ran while one was open for 5% -> 25% of each run, Pallas kernels for 0% -> 0%
where the time goes in v1:
time: 834 us; the launch traced here: 829 us
  matrix products  284 us (34%)
  other arithmetic  168 us (20%)
  blocking collectives  158 us (19%)
  local copies, waits for them, and re-layouts  148 us (18%)
  waiting for transfers between devices  52.4 us (6%)
  between operations  15.6 us (2%)
    dot_general x3, matrix products, mixer(): jnp.einsum('khts,kshp->kthp', weights, head_values, precision=highest)  105 us
    psum x1, blocking collectives, local(): lax.psum((grad_pre_gain, grad_conv_state, grad_conv_state_bias), ('dp', '...  87.2 us
    psum x1, blocking collectives, local(): lax.psum((grad_conv_value, grad_conv_value_bias, grad_step_bias, grad_dec...  64.4 us
    psum x1, waiting for transfers between devices, summed(): return lax.psum(array.astype(jnp.bfloat16), 'dp').astype(jnp.float32)  52.3 us
    dot_general x5, matrix products, dot_outer(): lax.dot_general(left, right, (((1,), (1,)), ((), ())), preferred_element_...  41.4 us
    reshape x4, local copies, waits for them, and re-layouts, mixer(): head_values = conv_out.reshape(block_count, BLOCK, head_count, head_width)  40.7 us
    reshape x4, local copies, waits for them, and re-layouts, mixer(): mixed_out = mixed_out.reshape(length, head_count * head_width)  37.1 us
    dot_general x3, matrix products, mixer(): jnp.einsum('ksn,khs,kshp->khnp', writer, tail_weight, head_values, precis...  36.9 us
  transfers between devices with their start and end apart: 4, of which 1 were waited for; matrix products, arithmetic and copies ran while one was open for 25% of the time, Pallas kernels for 0%

profile of v1, /device:TPU:0, one launch (start us, length us, event | category | flops | bytes accessed | tf_op | source)
XLA Modules:
  0.0 828.5 jit_solution(9986737274814158770)
XLA Ops:
  9.3 2.6 fusion.31
  12.5 2.7 fusion.33
  18.6 2.6 reduce-window.14
  21.6 7.8 fusion.142
  29.5 6.6 fusion.49
  36.1 6.6 copy.193
  42.6 10.0 %reshape.694 = f32[1,4,256,24,64]{4,3,2,1,0:T(8,128)} reshape(f32[1,1024,1536]{2,1,0:T(8,128)} %get-tuple-element.381) | data formatting | bytes 12582912 | tf_op jit(solution)/shard_map/jvp(vmap())/reshape | solution.py:56
  54.6 3.0 fusion.143
  61.2 6.9 fusion.146
  68.1 8.1 reshape.652
  76.8 10.4 %fusion.83 = f32[4,1,24,128,64]{3,4,2,0,1:T(8,128)} fusion(f32[4,256,128,1]{2,1,3,0:T(8,128)S(1)} %bitcast.287, f32[4,256,24,64]{1,0,3,2:T(4,128)} %reshape.652, f32[4,256,24]{1,2,0:T(8,128)S(1)} %get-tuple-element.415), kind=kOutput, calls=%fused_computation.126 | convolution fusion | flops 2417491968 | bytes 10059776 | tf_op jit(solution)/shard_map/jvp(vmap(ksn,khs,kshp->khnp))/dot_general | solution.py:67
  87.2 3.4 broadcast.235.clone
  90.6 23.5 %while.34 = (s32[]{:T(128)}, f32[1,24,128,64]{3,2,1,0:T(8,128)S(1)}, f32[4,1,24,128,64]{4,3,2,1,0:T(8,128)}, f32[4,1,24,1,1]{2,4,3,1,0:T(1,128)S(1)}, f32[4,1,24...) while((s32[]{:T(128)}, f32[1,24,128,64]{3,2,1,0:T(8,128)S(1)}, ...), condition=%wide.region_4.5_spmd.clone, body=%wide.region_3.4_spmd.clone.sunk | while | flops 786435 | bytes 7865752 | solution.py:77
  114.2 6.2 copy.205
  121.4 8.8 %fusion.145 = f32[4,256,1536]{1,2,0} fusion(f32[4,256,128]{2,1,0:T(8,128)S(1)} %bitcast.292, f32[4,128,1536]{1,2,0:T(8,128)} %bitcast.295), kind=kOutput, calls=%fused_computation.219 | convolution fusion | flops 2415919104 | bytes 9961472
  130.2 9.8 %copy.207 = f32[1,4,256,24,64]{2,4,3,1,0:T(8,128)} copy(f32[1,4,256,24,64]{4,3,2,1,0:T(8,128)} %reshape.694) | data formatting | bytes 12582912 | tf_op jit(solution)/shard_map/jvp(vmap())/reshape | solution.py:56
  140.6 33.5 %fusion.42 = f32[1,4,256,24,64]{2,4,3,1,0:T(8,128)} fusion(f32[1,4,256,24,64]{2,4,3,1,0:T(8,128)} %copy.207, f32[4,256,24,64]{1,3,2,0:T(8,128)} %bitcast.281, f32[24]{0:T(128)S(1)} %copy-done.81, f32[4,256,24]{1,2,0:T(8,128)S(1)} %bitcast.304, f32[4,24,256]{2,1,0:T(8,128)S(1)} %copy-done.38, f32[256,256]{1,0:T(8,128)S(1)} %copy-done.34, ...), kind=kOutput, calls=%fused_computation.71 | convolution fusion | flops 4869586944 | bytes 26837088 | tf_op jit(solution)/shard_map/jvp(vmap(khts,kshp->kthp))/dot_general | solution.py:65
  174.1 9.7 %copy.254 = f32[1,4,256,24,64]{4,3,2,1,0:T(8,128)} copy(f32[1,4,256,24,64]{2,4,3,1,0:T(8,128)} %fusion.42) | data formatting | bytes 12582912 | tf_op jit(solution)/shard_map/jvp(vmap())/reshape | solution.py:83
  183.8 11.1 %reshape.695 = f32[1024,1536]{1,0:T(8,128)} reshape(f32[1,4,256,24,64]{4,3,2,1,0:T(8,128)} %copy.254) | data formatting | bytes 12582912 | tf_op jit(solution)/shard_map/jvp(vmap())/reshape | solution.py:83
  195.0 14.5 %multiply_reduce_fusion.10 = (f32[1024]{0:T(1024)S(1)}, f32[1024]{0:T(1024)S(1)}, f32[1024,1536]{1,0:T(8,128)}, f32[1024,1536]{1,0:T(8,128)}) fusion(f32[1536]{0:T(1024)S(1)} %copy-done.58, f32[1024,1536]{1,0:T(8,128)} %reshape.695, f32[1024,1536]{1,0:T(8,128)} %fusion.146, bf16[1024,1536]{1,0:T(8,128)(2,1)} %param.21, bf16[1536,1536]{1,0:T(8,128)(2,1)} %param.35), kind=kOutput, calls=%fused_computation.91 | convolution fusion | flops 4847564800 | bytes 33044480 | tf_op jit(solution)/shard_map/dot_general | solution.py:98
  209.5 6.0 psum.105
  215.5 13.8 %fusion.43 = (f32[1536]{0:T(1024)}, f32[1024,1536]{1,0:T(8,128)}) fusion(f32[1,1024,1536]{2,1,0:T(8,128)} %get-tuple-element.382, f32[1024,1536]{1,0:T(8,128)} %fusion.146, f32[1024]{0:T(1024)S(1)} %bitcast.325, f32[1024,1536]{1,0:T(8,128)} %get-tuple-element.376, f32[1024]{0:T(1024)S(1)} %multiply_multiply_fusion.1, f32[1024,1536]{1,0:T(8,128)} %get-tuple-element.412, ...), kind=kLoop, calls=%fused_computation.73 | loop fusion | flops 26737152 | bytes 31481856 | tf_op jit(solution)/shard_map/transpose(jvp(vmap()))/reduce_sum | solution.py:82
  229.3 6.6 copy.211
  235.9 8.1 reshape.669
  244.0 8.1 reshape.672
  252.1 22.8 %fusion.89 = f32[4,256,128]{2,1,0:T(8,128)S(1)} fusion(f32[4,256,24,64]{1,0,3,2:T(4,128)} %reshape.669, f32[4,256,24]{1,2,0:T(8,128)S(1)} %bitcast.305, f32[4,1,24,128,64]{4,3,2,1,0:T(8,128)} %get-tuple-element.534), kind=kOutput, calls=%fused_computation.131 | convolution fusion | flops 2417491968 | bytes 10059776 | tf_op jit(solution)/shard_map/transpose(jvp(vmap(ktn,khnp->kthp)))/dot_general | solution.py:79
  275.0 45.6 %fusion.11 = (f32[4,24,256]{2,1,0:T(8,128)}, f32[4,24,256]{2,1,0:T(8,128)}, f32[4,24,256]{2,1,0:T(8,128)}, f32[4,256,256]{2,1,0:T(8,128)S(1)}) fusion(f32[4,24,256]{2,1,0:T(8,128)S(1)} %copy-done.38, f32[256,256]{1,0:T(8,128)S(1)} %copy-done.34, f32[4,24,256]{2,1,0:T(8,128)S(1)} %copy-done.41, f32[4,256,256]{2,1,0:T(8,128)S(1)} %copy-done.27, ...), kind=kOutput, calls=%fused_computation.30 | convolution fusion | flops 4925874176 | bytes 15499264 | tf_op jit(solution)/shard_map/transpose(jvp(vmap(khts,kshp->kthp)))/dot_general | solution.py:65
  324.4 7.7 fusion.86
  332.0 3.4 broadcast.235
  335.4 26.2 %while.35 = (s32[]{:T(128)}, f32[1,24,128,64]{3,2,1,0:T(8,128)S(1)}, f32[4,1,24,128,64]{4,3,2,1,0:T(8,128)}, f32[4,1,24]{2,1,0:T(1,128)S(1)}, f32[4,1,24,128,64]...) while((s32[]{:T(128)}, ...), condition=%wide.region_10.11_spmd.clone, body=%wide.region_8.10_spmd.clone.sunk | while | flops 1179628 | bytes 8652312 | solution.py:77
  339.7 2.4 fusion.193
  346.2 2.4 fusion.193
  352.8 2.4 fusion.193
  359.3 2.4 fusion.193
  361.7 16.0 %fusion.97 = f32[1,4,256,128]{2,3,1,0:T(8,128)} fusion(f32[1,4,256,128]{2,3,1,0:T(8,128)} %convolution_bitcast_fusion, f32[4,256,24,64]{1,0,3,2:T(4,128)} %reshape.652, f32[4,256,24]{1,2,0:T(8,128)S(1)} %copy-done.30, f32[4,1,24,128,64]{4,3,2,1,0:T(8,128)} %get-tuple-element.193), kind=kOutput, calls=%fused_computation.133 | convolution fusion | flops 2417623040 | bytes 10584064 | tf_op jit(solution)/shard_map/transpose(jvp(vmap(ksn,khs,kshp->khnp)))/dot_general | solution.py:67
  379.8 2.5 multiply_reduce_fusion.13
  386.2 11.3 %multiply_reduce_fusion.3 = (f32[1536]{0:T(1024)S(1)}, bf16[1024,1536]{1,0:T(8,128)(2,1)S(1)}) fusion(f32[1024,1536]{1,0:T(8,128)} %get-tuple-element.412, f32[1024,1536]{1,0:T(8,128)} %get-tuple-element.376, f32[1024]{0:T(1024)S(1)} %bitcast.322, f32[1024,1536]{1,0:T(8,128)} %fusion.146, f32[1024,1536]{1,0:T(8,128)} %reshape.695, f32[1024]{0:T(1024)S(1)} %bitcast.326, ...), kind=kLoop, calls=%fused_computation.80 | loop fusion | flops 31455744 | bytes 28336128 | tf_op jit(solution)/shard_map/reduce_sum | solution.py:171
  397.6 11.7 %convolution_convert_fusion = bf16[1536,1536]{1,0:T(8,128)(2,1)} fusion(bf16[1024,1536]{1,0:T(8,128)(2,1)S(1)} %copy-done.17, f32[1024,1536]{1,0:T(8,128)} %get-tuple-element.376, f32[1024]{0:T(1024)S(1)} %bitcast.323, f32[1536]{0:T(1024)S(1)} %copy-done.59), kind=kOutput, calls=%fused_computation.47 | convolution fusion | flops 4838916096 | bytes 14166016 | tf_op jit(solution)/shard_map/dot_general | solution.py:92
  409.3 4.8 multiply_reduce_fusion.8
  414.3 10.5 %fusion.80 = f32[4,256,24,64]{1,3,2,0:T(8,128)S(1)} fusion(f32[4,256,128,1]{2,1,3,0:T(8,128)S(1)} %bitcast.290, f32[4,1,24,128,64]{4,3,2,1,0:T(8,128)S(1)} %bitcast.280), kind=kOutput, calls=%fused_computation.123 | convolution fusion | flops 2415919104 | bytes 9961472 | tf_op jit(solution)/shard_map/transpose(jvp(vmap(ksn,khs,kshp->khnp)))/dot_general | solution.py:67
  424.8 2.7 copy-done.8
  427.5 26.1 %bitcast_add_fusion.2 = f32[1,4,256,24,64]{2,4,3,1,0:T(8,128)} fusion(f32[4,256,24,64]{1,3,2,0:T(8,128)S(1)} %fusion.80, f32[4,256,24,64]{1,0,3,2:T(4,128)S(1)} %bitcast.278, f32[24]{0:T(128)S(1)} %copy-done.82, f32[4,256,24]{1,2,0:T(8,128)S(1)} %copy-done.30, f32[4,24,256]{2,1,0:T(8,128)S(1)} %copy-done.39, f32[256,256]{1,0:T(8,128)S(1)} %copy-done.35, ...), kind=kOutput, calls=%fused_computation.69 | convolution fusion | flops 4869586944 | bytes 26837088 | tf_op jit(solution)/shard_map/transpose(jvp(vmap(khts,kshp->kthp)))/dot_general | solution.py:65
  453.6 10.1 %multiply_reduce_fusion.2 = f32[4,256,24]{1,0,2:T(4,128)S(1)} fusion(f32[4,256,24,64]{1,0,3,2:T(4,128)S(1)} %bitcast.274, f32[4,256,24,64]{1,3,2,0:T(8,128)} %copy-done.8), kind=kLoop, calls=%fused_computation.79 | loop fusion | flops 3121152 | bytes 12681216
  463.8 6.9 convolution_convert_fusion.2
  472.3 10.2 %reduce-window.16 = f32[1,4,24,2,128]{4,2,3,1,0:T(8,128)S(1)} reduce-window(f32[1,4,24,2,128]{4,2,3,1,0:T(8,128)S(1)} %copy.227, f32[]{:T(128)} %constant.99.clone.1), window={size=1x1x1x1x128 pad=0_0x0_0x0_0x0_0x0_127}, to_apply=%region_16.17 | reduce-window | flops 3121152 | bytes 196612 | tf_op jit(solution)/shard_map/reduce-window.2
  483.2 9.8 %copy.256 = f32[1,4,256,24,64]{4,3,2,1,0:T(8,128)} copy(f32[1,4,256,24,64]{2,4,3,1,0:T(8,128)} %bitcast_add_fusion.2) | data formatting | bytes 12582912 | tf_op jit(solution)/shard_map/transpose(jvp(vmap()))/reshape | solution.py:56
  493.0 11.2 %reshape.696 = f32[1,1024,1536]{2,1,0:T(8,128)} reshape(f32[1,4,256,24,64]{4,3,2,1,0:T(8,128)} %copy.256) | data formatting | bytes 12582912 | tf_op jit(solution)/shard_map/transpose(jvp(vmap()))/reshape | solution.py:56
  504.2 14.3 %multiply_reduce_fusion.6 = (f32[1536]{0:T(1024)S(1)}, f32[1536]{0:T(1024)S(1)}, f32[1536]{0:T(1024)S(1)}, f32[1536]{0:T(1024)S(1)}, f32[1536]{0:T(1024)S(1)}, /*index=5*/f32[1,1024,1536]{2,1,0:T(8,128)S(1)}) fusion(f32[1,1024,1536]{2,1,0:T(8,128)} %bitcast.272, f32[1024,1536]{1,0:T(8,128)} %copy-done.2, f32[1,1024,1536]{2,1,0:T(8,128)} %get-tuple-element.382, ...), kind=kLoop, calls=%fused_computation.83 | loop fusion | flops 28303872 | bytes 31488000 | tf_op jit(solution)/shard_map/transpose(jvp(vmap()))/reduce_sum | solution.py:25
  518.5 6.0 broadcast_multiply_fusion
  524.5 6.3 fusion.66
  530.9 6.8 convolution_convert_fusion.1
  539.1 8.1 fusion.147
  547.2 9.7 %fusion.148 = f32[1024,1536]{1,0:T(8,128)} fusion(bf16[1024,1536]{1,0:T(8,128)(2,1)S(1)} %copy-done.19, bf16[1536,1536]{1,0:T(8,128)(2,1)} %param.24), kind=kOutput, calls=%fused_computation.222 | convolution fusion | flops 4831838208 | bytes 14155776 | tf_op jit(solution)/shard_map/dot_general | solution.py:98
  557.9 8.1 fusion.141
  568.1 9.1 %convolution_convert_fusion.3 = bf16[1024,1536]{1,0:T(8,128)(2,1)} fusion(bf16[1536,1536]{1,0:T(8,128)(2,1)} %param.35, f32[1024,1536]{1,0:T(8,128)S(1)} %bitcast.284, f32[1024]{0:T(1024)S(1)} %bitcast.324, f32[1536]{0:T(1024)S(1)} %copy-done.59), kind=kOutput, calls=%fused_computation.112 | convolution fusion | flops 4838129664 | bytes 14166016 | tf_op jit(solution)/shard_map/dot_general | solution.py:88
  577.5 64.4 %all-reduce.23 = (f32[4,1536]{1,0:T(4,128)}, f32[1536]{0:T(1024)}, f32[24]{0:T(128)}, f32[24]{0:T(128)}, f32[24]{0:T(128)}, /*index=5*/f32[1536]{0:T(1024)}) all-reduce(f32[4,1536]{1,0:T(4,128)S(1)} %pad_add_fusion.6, f32[1536]{0:T(1024)S(1)} %get-tuple-element.312, ...), channel_id=1, replica_groups=mesh['dp'=16,'tensor'=2] {'dp'}, use_global_device_ids=true, to_apply=%region_30.31 | all-reduce | flops 9288 | bytes 74304 | tf_op jit(solution)/shard_map/psum | solution.py:226
  642.0 2.4 convert_element_type.99
  644.4 7.6 fusion.40
  652.0 87.2 %all-reduce.22 = (f32[1536]{0:T(1024)}, f32[4,256]{1,0:T(4,128)}, f32[256]{0:T(256)}) all-reduce(f32[1536]{0:T(1024)S(1)} %get-tuple-element.316, f32[4,256]{1,0:T(4,128)S(1)} %pad_add_fusion.7, f32[256]{0:T(256)S(1)} %copy-done.75), channel_id=1, replica_groups=mesh['dp'=16,'tensor'=2] {'dp','tensor'}, use_global_device_ids=true, to_apply=%region_21.22 | all-reduce | flops 2816 | bytes 22528 | tf_op jit(solution)/shard_map/psum | solution.py:216
  739.2 10.6 %fusion.37 = (f32[1024,1536]{1,0:T(8,128)}, bf16[1024,1536]{1,0:T(8,128)(2,1)}) fusion(bf16[1024,1536]{1,0:T(8,128)(2,1)} %param.20, bf16[1024,1536]{1,0:T(8,128)(2,1)} %param.21, bf16[1024,1536]{1,0:T(8,128)(2,1)} %collective-permute-done.1, bf16[1024,1536]{1,0:T(8,128)(2,1)} %get-tuple-element.413, f32[1024]{0:T(1024)S(1)} %get-tuple-element.317, ...), kind=kLoop, calls=%fused_computation.61 | loop fusion | flops 26738688 | bytes 28329984 | tf_op jit(solution)/shard_map/sub | solution.py:201
  749.8 52.3 %all-reduce.30.cloned.1.call-done = (bf16[1536,1536]{1,0:T(8,128)(2,1)}, bf16[1536,1536]{1,0:T(8,128)(2,1)}, bf16[1536,24]{0,1:T(8,128)(2,1)}, bf16[1536,1536]{1,0:T(8,128)(2,1)}) async-done(((bf16[1536,1536]{1,0:T(8,128)(2,1)}, bf16[1536,1536]{1,0:T(8,128)(2,1)}, bf16[1536,24]{0,1:T(8,128)(2,1)}, bf16[1536,1536]{1,0:T(8,128)(2,1)}), (bf16[1536,1536]{1,0:T(8,128)(2,1)}, bf16[1536,1536]{1,0:T(8,128)(2,1)}, ...) | async-done | bytes 14229520 | tf_op jit(solution)/shard_map/psum | solution.py:207
  803.8 7.6 convert_element_type.93
  811.4 5.1 convert_element_type.95
  816.4 5.1 convert_element_type.101
  (335 shorter events, 72.7 us)
Async XLA Ops:
  7.2 47.3 %copy-start = (bf16[1536,256]{1,0:T(8,128)(2,1)S(1)}, bf16[1536,256]{1,0:T(8,128)(2,1)}, u32[]{:S(2)}) copy-start(bf16[1536,256]{1,0:T(8,128)(2,1)} %param.26) | copy-start | bytes 2359300
  7.2 9.7 %copy-start.32 = (bf16[1536,24]{0,1:T(8,128)(2,1)S(1)}, bf16[1536,24]{0,1:T(8,128)(2,1)}, u32[]{:S(2)}) copy-start(bf16[1536,24]{0,1:T(8,128)(2,1)} %param.25) | copy-start | bytes 221188
  7.2 9.7 %copy-start.79 = (f32[24]{0:T(128)S(1)}, f32[24]{0:T(128)}, u32[]{:S(2)}) copy-start(f32[24]{0:T(128)} %param.31) | copy-start | bytes 292
  7.2 634.8 %all-reduce.28.cloned.1.call-start = ((), (), s32[]{:S(2)}) async-start(), calls=%async_computation | async-start | bytes 1572864 | tf_op jit(solution)/shard_map/psum | solution.py:213
  9.3 9.1 %copy-start.73 = (f32[24]{0:T(128)}, f32[24]{0:T(128)S(1)}, u32[]{:S(2)}) copy-start(f32[24]{0:T(128)S(1)} %exponential_negate_fusion) | copy-start | bytes 292
  12.5 8.9 %copy-start.60 = (f32[4,1536]{1,0:T(4,128)S(1)}, f32[4,1536]{1,0:T(4,128)}, u32[]{:S(2)}) copy-start(f32[4,1536]{1,0:T(4,128)} %param.27) | copy-start | bytes 73732
  21.5 7.9 copy-start.45
  21.5 7.9 copy-start.47
  21.6 7.9 copy-start.49
  42.6 10.0 %copy-start.78 = (f32[4,256]{1,0:T(4,128)S(1)}, f32[4,256]{1,0:T(4,128)}, u32[]{:S(2)}) copy-start(f32[4,256]{1,0:T(4,128)} %param.29) | copy-start | bytes 12292
  61.2 15.6 %copy-start.11 = (f32[1,1024,128]{2,1,0:T(8,128)}, f32[1,1024,128]{2,1,0:T(8,128)S(1)}, u32[]{:S(2)}) copy-start(f32[1,1024,128]{2,1,0:T(8,128)S(1)} %get-tuple-element.397) | copy-start | bytes 1572868
  76.8 13.8 %copy-start.29 = (f32[4,256,24]{1,2,0:T(8,128)}, f32[4,256,24]{1,2,0:T(8,128)S(1)}, u32[]{:S(2)}) copy-start(f32[4,256,24]{1,2,0:T(8,128)S(1)} %get-tuple-element.415) | copy-start | bytes 294916
  121.4 18.6 %copy-start.26 = (f32[4,256,256]{2,1,0:T(8,128)}, f32[4,256,256]{2,1,0:T(8,128)S(1)}, u32[]{:S(2)}) copy-start(f32[4,256,256]{2,1,0:T(8,128)S(1)} %fusion.144) | copy-start | bytes 3145732
  130.2 10.5 %copy-start.34 = (f32[256,256]{1,0:T(8,128)S(1)}, f32[256,256]{1,0:T(8,128)}, u32[]{:S(2)}) copy-start(f32[256,256]{1,0:T(8,128)} %fusion.108) | copy-start | bytes 786436
  130.2 10.5 %copy-start.38 = (f32[4,24,256]{2,1,0:T(8,128)S(1)}, f32[4,24,256]{2,1,0:T(8,128)}, u32[]{:S(2)}) copy-start(f32[4,24,256]{2,1,0:T(8,128)} %get-tuple-element.416) | copy-start | bytes 294916
  130.2 10.5 %copy-start.81 = (f32[24]{0:T(128)S(1)}, f32[24]{0:T(128)}, u32[]{:S(2)}) copy-start(f32[24]{0:T(128)} %param.33) | copy-start | bytes 292
  183.8 11.1 %copy-start.58 = (f32[1536]{0:T(1024)S(1)}, f32[1536]{0:T(1024)}, u32[]{:S(2)}) copy-start(f32[1536]{0:T(1024)} %param.34) | copy-start | bytes 18436
  252.1 22.9 %copy-start.15 = (f32[1,4,256,24,64]{2,1,4,3,0:T(4,128)S(1)}, f32[1,4,256,24,64]{2,1,4,3,0:T(4,128)}, u32[]{:S(2)}) copy-start(f32[1,4,256,24,64]{2,1,4,3,0:T(4,128)} %reshape.672) | copy-start | bytes 18874372
  252.1 22.9 %copy-start.27 = (f32[4,256,256]{2,1,0:T(8,128)S(1)}, f32[4,256,256]{2,1,0:T(8,128)}, u32[]{:S(2)}) copy-start(f32[4,256,256]{2,1,0:T(8,128)} %copy-done.26) | copy-start | bytes 3145732
  252.1 22.9 %copy-start.41 = (f32[4,24,256]{2,1,0:T(8,128)S(1)}, f32[4,24,256]{2,1,0:T(8,128)}, u32[]{:S(2)}) copy-start(f32[4,24,256]{2,1,0:T(8,128)} %copy-done.40) | copy-start | bytes 294916
  252.1 22.9 %copy-start.53 = (pred[256,256]{1,0:T(8,128)(4,1)S(1)}, pred[256,256]{1,0:T(8,128)(4,1)}, u32[]{:S(2)}) copy-start(pred[256,256]{1,0:T(8,128)(4,1)} %broadcast_compare_fusion) | copy-start | bytes 196612
  275.0 49.4 %slice-start.2 = ((s8[6291456]{0:T(1024)(128)(4,1)}), s8[4194304]{0:T(1024)(128)(4,1)S(1)}, s32[]{:S(2)}) async-start(s8[6291456]{0:T(1024)(128)(4,1)} %bitcast.275), calls=%async_computation.4 | async-start | bytes 8388608
  275.0 49.4 %slice-start.3 = ((s8[6291456]{0:T(1024)(128)(4,1)}), s8[2097152]{0:T(1024)(128)(4,1)S(1)}, s32[]{:S(2)}) async-start(s8[6291456]{0:T(1024)(128)(4,1)} %bitcast.275), calls=%async_computation.5 | async-start | bytes 4194304
  324.4 11.1 %copy-start.1 = (f32[1,24,128,64]{3,2,1,0:T(8,128)S(1)}, f32[1,24,128,64]{3,2,1,0:T(8,128)}, u32[]{:S(2)}) copy-start(f32[1,24,128,64]{3,2,1,0:T(8,128)} %custom-call.1) | copy-start | bytes 2359300
  335.4 26.2 %copy-start.30 = (f32[4,256,24]{1,2,0:T(8,128)S(1)}, f32[4,256,24]{1,2,0:T(8,128)}, u32[]{:S(2)}) copy-start(f32[4,256,24]{1,2,0:T(8,128)} %copy-done.29) | copy-start | bytes 294916
  361.7 18.1 %copy-start.10 = (f32[1024,256]{1,0:T(8,128)S(1)}, f32[1024,256]{1,0:T(8,128)}, u32[]{:S(2)}) copy-start(f32[1024,256]{1,0:T(8,128)} %copy-done.9) | copy-start | bytes 3145732
  361.7 18.1 %copy-start.16 = (f32[1,1024,256]{2,1,0:T(8,128)S(1)}, f32[1,1024,256]{2,1,0:T(8,128)}, u32[]{:S(2)}) copy-start(f32[1,1024,256]{2,1,0:T(8,128)} %get-tuple-element.380) | copy-start | bytes 3145732
  361.7 18.1 %copy-start.23 = (f32[4,256,128]{2,1,0:T(8,128)S(1)}, f32[4,256,128]{2,1,0:T(8,128)}, u32[]{:S(2)}) copy-start(f32[4,256,128]{2,1,0:T(8,128)} %convolution_add_fusion) | copy-start | bytes 1572868
  386.1 416.0 %all-reduce.30.cloned.1.call-start = ((), (), s32[]{:S(2)}) async-start(), calls=%async_computation.1 | async-start | bytes 28459008 | tf_op jit(solution)/shard_map/psum | solution.py:207
  386.2 11.4 %copy-start.17 = (bf16[1024,1536]{1,0:T(8,128)(2,1)S(1)}, bf16[1024,1536]{1,0:T(8,128)(2,1)}, u32[]{:S(2)}) copy-start(bf16[1024,1536]{1,0:T(8,128)(2,1)} %param.21) | copy-start | bytes 9437188
  386.2 23.1 %slice-start.4 = ((s8[6291456]{0:T(1024)(128)(4,1)}), s8[4194304]{0:T(1024)(128)(4,1)S(1)}, s32[]{:S(2)}) async-start(s8[6291456]{0:T(1024)(128)(4,1)} %bitcast.277), calls=%async_computation.6 | async-start | bytes 8388608
  386.2 28.0 %slice-start.6 = ((s8[6291456]{0:T(1024)(128)(4,1)}), s8[4194304]{0:T(1024)(128)(4,1)S(1)}, s32[]{:S(2)}) async-start(s8[6291456]{0:T(1024)(128)(4,1)} %bitcast.279), calls=%async_computation.8 | async-start | bytes 8388608
  397.5 66.2 %copy-start.20 = (bf16[1024,1536]{1,0:T(8,128)(2,1)}, bf16[1024,1536]{1,0:T(8,128)(2,1)S(1)}, u32[]{:S(2)}) copy-start(bf16[1024,1536]{1,0:T(8,128)(2,1)S(1)} %get-tuple-element.386) | copy-start | bytes 9437188
  397.5 11.8 %slice-start.5 = ((s8[6291456]{0:T(1024)(128)(4,1)}), s8[2097152]{0:T(1024)(128)(4,1)S(1)}, s32[]{:S(2)}) async-start(s8[6291456]{0:T(1024)(128)(4,1)} %bitcast.277), calls=%async_computation.7 | async-start | bytes 4194304
  397.5 16.6 %slice-start.7 = ((s8[6291456]{0:T(1024)(128)(4,1)}), s8[2097152]{0:T(1024)(128)(4,1)S(1)}, s32[]{:S(2)}) async-start(s8[6291456]{0:T(1024)(128)(4,1)} %bitcast.279), calls=%async_computation.9 | async-start | bytes 4194304
  414.2 13.3 %copy-start.28 = (f32[4,256,256]{2,1,0:T(8,128)S(1)}, f32[4,256,256]{2,1,0:T(8,128)}, u32[]{:S(2)}) copy-start(f32[4,256,256]{2,1,0:T(8,128)} %copy-done.26) | copy-start | bytes 3145732
  414.2 13.3 %copy-start.35 = (f32[256,256]{1,0:T(8,128)S(1)}, f32[256,256]{1,0:T(8,128)}, u32[]{:S(2)}) copy-start(f32[256,256]{1,0:T(8,128)} %fusion.108) | copy-start | bytes 786436
  414.2 13.3 %copy-start.39 = (f32[4,24,256]{2,1,0:T(8,128)S(1)}, f32[4,24,256]{2,1,0:T(8,128)}, u32[]{:S(2)}) copy-start(f32[4,24,256]{2,1,0:T(8,128)} %get-tuple-element.416) | copy-start | bytes 294916
  414.2 13.3 %copy-start.42 = (f32[4,24,256]{2,1,0:T(8,128)S(1)}, f32[4,24,256]{2,1,0:T(8,128)}, u32[]{:S(2)}) copy-start(f32[4,24,256]{2,1,0:T(8,128)} %copy-done.40) | copy-start | bytes 294916
  414.3 13.2 %copy-start.54 = (pred[256,256]{1,0:T(8,128)(4,1)S(1)}, pred[256,256]{1,0:T(8,128)(4,1)}, u32[]{:S(2)}) copy-start(pred[256,256]{1,0:T(8,128)(4,1)} %broadcast_compare_fusion) | copy-start | bytes 196612
  414.3 13.2 %copy-start.82 = (f32[24]{0:T(128)S(1)}, f32[24]{0:T(128)}, u32[]{:S(2)}) copy-start(f32[24]{0:T(128)} %param.33) | copy-start | bytes 292
  414.3 39.3 %slice-start = ((s8[6291456]{0:T(1024)(128)(4,1)}), s8[4194304]{0:T(1024)(128)(4,1)S(1)}, s32[]{:S(2)}) async-start(s8[6291456]{0:T(1024)(128)(4,1)} %bitcast.273), calls=%async_computation.2 | async-start | bytes 8388608
  427.5 26.1 %slice-start.1 = ((s8[6291456]{0:T(1024)(128)(4,1)}), s8[2097152]{0:T(1024)(128)(4,1)S(1)}, s32[]{:S(2)}) async-start(s8[6291456]{0:T(1024)(128)(4,1)} %bitcast.273), calls=%async_computation.3 | async-start | bytes 4194304
  453.6 10.1 %copy-start.6 = (bf16[1024,1536]{1,0:T(8,128)(2,1)S(1)}, bf16[1024,1536]{1,0:T(8,128)(2,1)}, u32[]{:S(2)}) copy-start(bf16[1024,1536]{1,0:T(8,128)(2,1)} %copy-done.3) | copy-start | bytes 9437188
  463.8 8.1 copy-start.43
  504.2 14.3 %copy-start.46 = (f32[1536]{0:T(1024)S(1)}, f32[1536]{0:T(1024)}, u32[]{:S(2)}) copy-start(f32[1536]{0:T(1024)} %copy-done.45) | copy-start | bytes 18436
  504.2 14.3 %copy-start.48 = (f32[1536]{0:T(1024)S(1)}, f32[1536]{0:T(1024)}, u32[]{:S(2)}) copy-start(f32[1536]{0:T(1024)} %copy-done.47) | copy-start | bytes 18436
  504.2 14.3 %copy-start.50 = (f32[1536]{0:T(1024)S(1)}, f32[1536]{0:T(1024)}, u32[]{:S(2)}) copy-start(f32[1536]{0:T(1024)} %copy-done.49) | copy-start | bytes 18436
  504.2 14.3 %copy-start.52 = (f32[1536]{0:T(1024)S(1)}, f32[1536]{0:T(1024)}, u32[]{:S(2)}) copy-start(f32[1536]{0:T(1024)} %copy-done.51) | copy-start | bytes 18436
  539.1 8.1 copy-start.19
  547.1 9.7 %copy-start.33 = (bf16[1536,24]{0,1:T(8,128)(2,1)S(1)}, bf16[1536,24]{0,1:T(8,128)(2,1)}, u32[]{:S(2)}) copy-start(bf16[1536,24]{0,1:T(8,128)(2,1)} %param.25) | copy-start | bytes 221188
  556.9 11.2 %slice-start.8 = ((s8[6291456]{0:T(1024)(128)(4,1)}), s8[4194304]{0:T(1024)(128)(4,1)S(1)}, s32[]{:S(2)}) async-start(s8[6291456]{0:T(1024)(128)(4,1)} %bitcast.283), calls=%async_computation.10 | async-start | bytes 8388608
  557.9 10.2 %slice-start.9 = ((s8[6291456]{0:T(1024)(128)(4,1)}), s8[2097152]{0:T(1024)(128)(4,1)S(1)}, s32[]{:S(2)}) async-start(s8[6291456]{0:T(1024)(128)(4,1)} %bitcast.283), calls=%async_computation.11 | async-start | bytes 4194304
  566.0 11.2 %copy-start.57 = (f32[1536]{0:T(1024)S(1)}, f32[1536]{0:T(1024)}, u32[]{:S(2)}) copy-start(f32[1536]{0:T(1024)} %get-tuple-element.368) | copy-start | bytes 18436
  566.0 11.5 %copy-start.83 = (f32[24]{0:T(128)S(1)}, f32[24]{0:T(128)}, u32[]{:S(2)}) copy-start(f32[24]{0:T(128)} %param.32) | copy-start | bytes 292
  566.0 76.0 %copy-start.76 = (f32[256]{0:T(256)S(1)}, f32[256]{0:T(256)}, u32[]{:S(2)}) copy-start(f32[256]{0:T(256)} %get-tuple-element.320) | copy-start | bytes 3076
  566.0 76.0 %copy-start.77 = (f32[256]{0:T(256)S(1)}, f32[256]{0:T(256)}, u32[]{:S(2)}) copy-start(f32[256]{0:T(256)} %get-tuple-element.322) | copy-start | bytes 3076
  566.0 78.4 %copy-start.44 = (f32[1536]{0:T(1024)S(1)}, f32[1536]{0:T(1024)}, u32[]{:S(2)}) copy-start(f32[1536]{0:T(1024)} %param.22) | copy-start | bytes 18436
  566.0 78.4 %copy-start.56 = (f32[1024]{0:T(1024)S(1)}, f32[1024]{0:T(1024)}, u32[]{:S(2)}) copy-start(f32[1024]{0:T(1024)} %copy-done.55) | copy-start | bytes 12292
  566.0 78.4 %collective-permute-start.1 = (bf16[1024,1536]{1,0:T(8,128)(2,1)}, bf16[1024,1536]{1,0:T(8,128)(2,1)}, u32[]{:S(2)}, u32[]{:S(2)}) collective-permute-start(bf16[1024,1536]{1,0:T(8,128)(2,1)} %get-tuple-element.413), channel_id=1, source_target_pairs={{0,1},{1,0},{2,3},{3,2},{4,5},{5,4},{6,7},{7,6},{8,9},{9,8},{10,11... | collective-permute-start | bytes 9437192 | tf_op jit(solution)/shard_map/ppermute | solution.py:197
  577.2 162.0 %collective-permute-start = (bf16[1024,1536]{1,0:T(8,128)(2,1)}, bf16[1024,1536]{1,0:T(8,128)(2,1)}, u32[]{:S(2)}, u32[]{:S(2)}) collective-permute-start(bf16[1024,1536]{1,0:T(8,128)(2,1)} %convolution_convert_fusion.3), channel_id=1, source_target_pairs={{0,1},{1,0},{2,3},{3,2},{4,5},{5,4},{6,7},{7,6},{8,9},{9,8},{10,11... | collective-permute-start | bytes 9437192 | tf_op jit(solution)/shard_map/ppermute | solution.py:166
  644.4 94.8 %copy-start.63 = (f32[1024]{0:T(1024)S(1)}, f32[1024]{0:T(1024)}, u32[]{:S(2)}) copy-start(f32[1024]{0:T(1024)} %get-tuple-element.405) | copy-start | bytes 12292
  802.1 9.3 %slice-start.12 = ((s8[4718592]{0:T(1024)(128)(4,1)}), s8[4194304]{0:T(1024)(128)(4,1)S(1)}, s32[]{:S(2)}) async-start(s8[4718592]{0:T(1024)(128)(4,1)} %bitcast.300), calls=%async_computation.14 | async-start | bytes 8388608
  803.8 12.6 %slice-start.10 = ((s8[4718592]{0:T(1024)(128)(4,1)}), s8[4194304]{0:T(1024)(128)(4,1)S(1)}, s32[]{:S(2)}) async-start(s8[4718592]{0:T(1024)(128)(4,1)} %bitcast.298), calls=%async_computation.12 | async-start | bytes 8388608
  (40 other events, 229.2 us)
Sparse Core Ops, SparseCore 0:
  386.2 131.7 all-reduce.27
  539.2 262.8 all-reduce.29
